TPU v7x, 256 devices: a whole 4x4x8 slice. The times are simulated.
256 devices in a mesh: ia: 8 (over z_lo, core), ja: 32 (over y, x, z_hi).
Axes of the slice: x: 4, y: 4, z: 8 (z_hi: 2, z_lo: 4; z = z_hi * 4 + z_lo), core: 2. Of those that a mesh axis runs over, the one named last changes fastest.
Arguments:
- slab_rows: bfloat16 [256, 768, 128], P('ia', 'ja'), may hold values from -6 to 6
- column_rows: bfloat16 [512, 768, 128], P('ja', 'ia'), may hold values from -6 to 6
- pair_tile: bfloat16 [256, 512, 128], P('ia', 'ja'), may hold values from -6 to 6
- cotangent: bfloat16 [256, 512, 128], P('ia', 'ja'), may hold values from -6 to 6
- weights_left: bfloat16 [128, 256], replicated, may hold values from -0.5 to 0.5
- weights_right: bfloat16 [128, 256], replicated, may hold values from -0.5 to 0.5
- gate_weight: bfloat16 [128, 128], replicated, may hold values from -0.5 to 0.5
- out_weight: bfloat16 [128, 128], replicated, may hold values from -0.5 to 0.5
- input_gain: float32 [128], replicated, may hold values from 0.1 to 1.9
- input_bias: float32 [128], replicated, may hold values from -3 to 3
- update_gain: float32 [128], replicated, may hold values from 0.1 to 1.9
- update_bias: float32 [128], replicated, may hold values from -3 to 3
Outputs:
- update: bfloat16 [256, 512, 128], P('ia', 'ja')
- grad_slab: bfloat16 [256, 768, 128], P('ia', 'ja')
- grad_columns: bfloat16 [512, 768, 128], P('ja', 'ia')
- grad_tile: bfloat16 [256, 512, 128], P('ia', 'ja')
All inputs are finite; a program needn't handle non-finite values.
Results may differ from a plain program's by a relative error of at most 0.018.
Values may be sent and summed in bfloat16 or wider, within the bound.
No kernel may reach another device: no remote copies, remote signals or barrier semaphores. Data moves between devices by JAX's collectives and lax.ppermute only.
A program may use at most 128 MiB of HBM per device.

v0:
```python
import jax
import jax.numpy as jnp
from jax import lax
from jax.sharding import Mesh
from jax.sharding import PartitionSpec as P

JA = ("ja_0", "ja_1", "ja_2")
epsilon = 1e-05


def summed_rows(terms, axes):
    total = terms.astype(jnp.bfloat16)
    for axis in axes:
        total = lax.psum_scatter(total, axis, scatter_dimension=0, tiled=True)
    return total.astype(jnp.float32)


def in_blocks(array, dim, devices):
    before, after = (array.shape[:dim], array.shape[dim + 1 :])
    return jnp.moveaxis(array.reshape(*before, devices, -1, *after), dim, 0)


def sent_and_summed(array, axis, dim):
    devices = lax.axis_size(axis)
    blocks = lax.all_to_all(in_blocks(array, dim, devices), axis, 0, 0, tiled=True)
    return jnp.sum(blocks.astype(jnp.float32), axis=0)


def normalize(values, gain, bias):
    values = values.astype(jnp.float32)
    centre = jnp.mean(values, axis=-1, keepdims=True)
    shifted = values - centre
    inverse = lax.rsqrt(jnp.mean(shifted * shifted, axis=-1, keepdims=True) + epsilon)
    scaled = shifted * inverse
    return (scaled * gain + bias, scaled, inverse)


def norm_back(scaled, inverse, grad_out, gain):
    grad_hat = grad_out * gain
    first_mean = jnp.mean(grad_hat, axis=-1, keepdims=True)
    second_mean = jnp.mean(grad_hat * scaled, axis=-1, keepdims=True)
    return inverse * (grad_hat - first_mean - scaled * second_mean)


def project(rows, weights, input_gain, input_bias):
    normed, scaled, inverse = normalize(rows, input_gain, input_bias)
    hidden = jnp.dot(normed.astype(jnp.bfloat16), weights, preferred_element_type=jnp.float32)
    half_width = weights.shape[1] // 2
    linear = hidden[..., :half_width]
    sigma = jax.nn.sigmoid(hidden[..., half_width:])
    return ((sigma * linear).astype(jnp.bfloat16), linear, sigma, scaled, inverse)


def project_back(grad_edge, linear, sigma, scaled, inverse, weights, input_gain):
    joined = jnp.concatenate(
        [grad_edge * sigma, grad_edge * linear * sigma * (1.0 - sigma)], axis=-1
    )
    grad_norm = jnp.dot(joined.astype(jnp.bfloat16), weights.T, preferred_element_type=jnp.float32)
    return norm_back(scaled, inverse, grad_norm, input_gain).astype(jnp.bfloat16)


def shards(
    slab_rows,
    column_rows,
    pair_tile,
    cotangent,
    weights_left,
    weights_right,
    gate_weight,
    out_weight,
    input_gain,
    input_bias,
    update_gain,
    update_bias,
):
    left, lin_left, sig_left, scaled_left, inv_left = project(
        slab_rows, weights_left, input_gain, input_bias
    )
    right, lin_right, sig_right, scaled_right, inv_right = project(
        column_rows, weights_right, input_gain, input_bias
    )
    left_whole = lax.all_gather(left, JA, axis=1, tiled=True)
    panel_piece = lax.all_gather(right, "ia", axis=1, tiled=True)
    left_slice = left_whole
    running = jnp.einsum(
        "ikc,jkc->ijc", left_slice, panel_piece, preferred_element_type=jnp.float32
    )
    tri_norm, tri_scaled, tri_inverse = normalize(running, update_gain, update_bias)
    outer = jnp.dot(tri_norm.astype(jnp.bfloat16), out_weight, preferred_element_type=jnp.float32)
    tile_norm, tile_scaled, tile_inverse = normalize(pair_tile, input_gain, input_bias)
    gate_linear = jnp.dot(
        tile_norm.astype(jnp.bfloat16), gate_weight, preferred_element_type=jnp.float32
    )
    gate = jax.nn.sigmoid(gate_linear)
    update = (gate * outer).astype(jnp.bfloat16)
    grad_update = cotangent.astype(jnp.float32)
    grad_outer = (grad_update * gate).astype(jnp.bfloat16)
    grad_gate = (grad_update * outer * gate * (1.0 - gate)).astype(jnp.bfloat16)
    grad_tnorm = jnp.dot(grad_outer, out_weight.T, preferred_element_type=jnp.float32)
    grad_tri = norm_back(tri_scaled, tri_inverse, grad_tnorm, update_gain).astype(jnp.bfloat16)
    grad_pnorm = jnp.dot(grad_gate, gate_weight.T, preferred_element_type=jnp.float32)
    grad_tile = norm_back(tile_scaled, tile_inverse, grad_pnorm, input_gain).astype(jnp.bfloat16)
    left_sums = summed_rows(
        jnp.einsum("ijc,jkc->kic", grad_tri, panel_piece, preferred_element_type=jnp.float32), JA
    )
    left_slice = left_whole
    right_sums = sent_and_summed(
        jnp.einsum("ijc,ikc->kjc", grad_tri, left_slice, preferred_element_type=jnp.float32).astype(
            jnp.bfloat16
        ),
        "ia",
        0,
    )
    grad_left = jnp.transpose(left_sums, (1, 0, 2))
    grad_right = jnp.transpose(right_sums, (1, 0, 2))
    grad_slab = project_back(
        grad_left, lin_left, sig_left, scaled_left, inv_left, weights_left, input_gain
    )
    grad_columns = project_back(
        grad_right, lin_right, sig_right, scaled_right, inv_right, weights_right, input_gain
    )
    return (update, grad_slab, grad_columns, grad_tile)


def solution(mesh):
    finer = Mesh(mesh.devices.reshape(mesh.shape["ia"], 4, 4, 2), ("ia", "ja_0", "ja_1", "ja_2"))
    in_specs = (
        P("ia", JA, None),
        P(JA, "ia", None),
        P("ia", JA, None),
        P("ia", JA, None),
        P(),
        P(),
        P(),
        P(),
        P(),
        P(),
        P(),
        P(),
    )
    out_specs = (P("ia", JA, None), P("ia", JA, None), P(JA, "ia", None), P("ia", JA, None))
    return jax.shard_map(
        shards, mesh=finer, in_specs=in_specs, out_specs=out_specs, check_vma=False
    )
```

profile of v0, /device:TPU:1, one launch (start us, length us, event | category | flops | bytes accessed | tf_op | source)
XLA Modules:
  0.0 401.9 jit_solution(11439921015196536878)
XLA Ops:
  7.3 1.3 convert_reduce_fusion.1
  8.6 1.6 fusion.14
  10.2 1.6 fusion.37
  11.9 1.1 copy-done.1
  13.0 1.0 multiply_convert_fusion.1
  14.0 0.2 convert_reduce_fusion.2
  14.2 0.3 fusion.36
  14.6 0.4 fusion.69
  15.0 0.9 copy-done.5
  15.9 0.8 multiply_convert_fusion.2
  16.8 0.2 reduce-scatter.6.cloned.1.call-start
  17.0 0.1 convert_reduce_fusion.3
  17.3 0.2 fusion.64
  17.7 0.6 copy-done.17
  18.3 0.3 fusion.2
  18.7 0.7 copy-done.9
  19.4 0.2 fusion.76
  19.6 1.4 copy.77
  21.0 39.5 %all-gather.3.cloned.1.call-done = bf16[16,768,128]{2,1,0:T(8,128)(2,1)} async-done(((bf16[16,96,128]{2,1,0:T(8,128)(2,1)}), bf16[16,768,128]{2,1,0:T(8,128)(2,1)}) %all-gather.3.cloned.1.call-update) | async-done | bytes 3145744 | tf_op jit(solution)/shard_map/all_gather | solution.py:83
  60.6 3.9 copy.74
  64.5 137.4 %all-gather.5.cloned.1.call-done = bf16[32,768,128]{2,1,0:T(8,128)(2,1)} async-done(((bf16[32,24,128]{2,1,0:T(8,128)(2,1)}), bf16[32,768,128]{2,1,0:T(8,128)(2,1)}) %all-gather.5.cloned.1.call-update) | async-done | bytes 6291472 | tf_op jit(solution)/shard_map/all_gather | solution.py:82
  201.9 41.8 %copy.75 = bf16[32,768,128]{0,1,2:T(8,128)(2,1)} copy(bf16[32,768,128]{2,1,0:T(8,128)(2,1)} %all-gather.5.cloned.1.call-done) | data formatting | bytes 12582912 | tf_op jit(solution)/shard_map/all_gather | solution.py:82
  243.7 10.1 %fusion.99 = (f32[32,16]{0,1:T(8,128)S(1)}, f32[32,16,128]{0,1,2:T(8,128)S(1)}) fusion(bf16[16,768,128]{1,0,2:T(8,128)(2,1)S(1)} %copy.74, bf16[32,768,128]{0,1,2:T(8,128)(2,1)} %copy.75), kind=kOutput, calls=%fused_computation.142 | convolution fusion | flops 100728320 | bytes 9701376 | tf_op jit(solution)/shard_map/ikc,jkc->ijc/dot_general | solution.py:85
  253.9 0.2 multiply_reduce_fusion.1
  254.1 0.3 multiply_reduce_fusion.2
  254.5 1.3 multiply_convert_fusion
  255.8 0.8 copy-done.4
  256.6 4.6 %convert_bitcast_fusion = bf16[768,32,128]{0,1,2:T(8,128)(2,1)} fusion(bf16[16,768,128]{1,0,2:T(8,128)(2,1)S(1)} %copy.74, bf16[32,16,128]{0,1,2:T(8,128)(2,1)S(1)} %get-tuple-element.14), kind=kOutput, calls=%fused_computation.1 | convolution fusion | flops 103809024 | bytes 9568256 | tf_op jit(solution)/shard_map/ijc,jkc->kic/dot_general | solution.py:104
  261.1 9.6 %copy.79 = bf16[768,32,128]{2,1,0:T(8,128)(2,1)} copy(bf16[768,32,128]{0,1,2:T(8,128)(2,1)} %convert_bitcast_fusion) | data formatting | bytes 12582912 | tf_op jit(solution)/shard_map/convert_element_type | solution.py:12
  270.7 14.0 %convert_bitcast_fusion.1 = bf16[768,16,128]{0,1,2:T(8,128)(2,1)S(1)} fusion(bf16[32,768,128]{0,1,2:T(8,128)(2,1)} %copy.75, bf16[32,16,128]{0,1,2:T(8,128)(2,1)} %copy-done.4), kind=kOutput, calls=%fused_computation.2 | convolution fusion | flops 102236160 | bytes 9568256 | tf_op jit(solution)/shard_map/ijc,ikc->kjc/dot_general | solution.py:108
  284.7 4.0 copy.82
  288.7 6.5 %all-to-all-start = ((bf16[8,96,16,128]{3,2,1,0:T(8,128)(2,1)}), bf16[8,96,16,128]{3,2,1,0:T(8,128)(2,1)}, u32[]{:S(2)}, u32[]{:S(2)}) async-start(bf16[8,96,16,128]{3,2,1,0:T(8,128)(2,1)} %bitcast.75), calls=%async_computation.2 | async-start | bytes 6291456 | tf_op jit(solution)/shard_map/all_to_all | solution.py:25
  295.2 37.4 %reduce-scatter.6.cloned.1.call-done = bf16[192,32,128]{2,1,0:T(8,128)(2,1)} async-done(((bf16[768,32,128]{2,1,0:T(8,128)(2,1)}), bf16[192,32,128]{2,1,0:T(8,128)(2,1)}) %reduce-scatter.6.cloned.1.call-update) | async-done | bytes 1572880 | tf_op jit(solution)/shard_map/reduce_scatter | solution.py:14
  332.6 0.3 reduce-scatter.10.cloned.1.call-start
  332.9 0.5 copy.76
  333.4 0.8 multiply_convert_fusion.3
  334.3 0.4 fusion.98
  335.0 1.0 fusion.63
  336.0 29.9 %all-to-all-done = bf16[8,96,16,128]{3,2,1,0:T(8,128)(2,1)} async-done(((bf16[8,96,16,128]{3,2,1,0:T(8,128)(2,1)}), bf16[8,96,16,128]{3,2,1,0:T(8,128)(2,1)}, u32[]{:S(2)}, u32[]{:S(2)}) %all-to-all-start) | async-done | bytes 3145760 | tf_op jit(solution)/shard_map/all_to_all | solution.py:25
  365.9 2.4 convert_reduce_fusion
  368.4 1.1 fusion.21
  369.5 2.0 copy.97
  371.6 2.1 fusion.96
  373.6 1.7 fusion.13
  375.3 17.2 %reduce-scatter.10.cloned.1.call-done = bf16[24,4096]{1,0:T(8,128)(2,1)} async-done(((bf16[48,4096]{1,0:T(8,128)(2,1)}), bf16[24,4096]{1,0:T(8,128)(2,1)}) %reduce-scatter.10.cloned.1.call-update) | async-done | bytes 196624
  392.5 1.1 fusion.45
  393.7 0.5 fusion.97
  394.2 1.2 fusion.35
  (101 shorter events, 1.1 us)
Async XLA Ops:
  7.2 3.0 copy-start
  7.2 7.4 %copy-start.31 = (f32[128]{0:T(128)S(1)}, f32[128]{0:T(128)}, u32[]{:S(2)}) copy-start(f32[128]{0:T(128)} %param.20) | copy-start | bytes 1540
  7.2 7.4 %copy-start.34 = (f32[128]{0:T(128)S(1)}, f32[128]{0:T(128)}, u32[]{:S(2)}) copy-start(f32[128]{0:T(128)} %param.21) | copy-start | bytes 1540
  7.2 6.8 %copy-start.8 = (bf16[32,24,128]{2,1,0:T(8,128)(2,1)S(1)}, bf16[32,24,128]{2,1,0:T(8,128)(2,1)}, u32[]{:S(2)}) copy-start(bf16[32,24,128]{2,1,0:T(8,128)(2,1)} %param.12) | copy-start | bytes 589828
  7.2 7.4 %copy-start.27 = (bf16[128,256]{1,0:T(8,128)(2,1)S(1)}, bf16[128,256]{1,0:T(8,128)(2,1)}, u32[]{:S(2)}) copy-start(bf16[128,256]{1,0:T(8,128)(2,1)} %param.16) | copy-start | bytes 196612
  7.2 53.3 %all-gather.3.cloned.1.call-start = ((), (), s32[]{:S(2)}) async-start(), calls=%async_computation.4 | async-start | bytes 3538944 | tf_op jit(solution)/shard_map/all_gather | solution.py:83
  8.6 1.6 copy-start.21
  10.2 1.7 copy-start.25
  10.2 6.8 %copy-start.12 = (bf16[32,16,128]{2,1,0:T(8,128)(2,1)S(1)}, bf16[32,16,128]{2,1,0:T(8,128)(2,1)}, u32[]{:S(2)}) copy-start(bf16[32,16,128]{2,1,0:T(8,128)(2,1)} %param.14) | copy-start | bytes 393220
  11.9 1.1 copy-start.1
  13.0 5.3 %copy-start.29 = (bf16[128,128]{1,0:T(8,128)(2,1)S(1)}, bf16[128,128]{1,0:T(8,128)(2,1)}, u32[]{:S(2)}) copy-start(bf16[128,128]{1,0:T(8,128)(2,1)} %param.18) | copy-start | bytes 98308
  13.0 6.4 %copy-start.13 = (bf16[32,16,128]{2,1,0:T(8,128)(2,1)S(1)}, bf16[32,16,128]{2,1,0:T(8,128)(2,1)}, u32[]{:S(2)}) copy-start(bf16[32,16,128]{2,1,0:T(8,128)(2,1)} %param.15) | copy-start | bytes 393220
  13.0 6.4 %copy-start.23 = (bf16[128,128]{1,0:T(8,128)(2,1)S(1)}, bf16[128,128]{1,0:T(8,128)(2,1)}, u32[]{:S(2)}) copy-start(bf16[128,128]{1,0:T(8,128)(2,1)} %param.19) | copy-start | bytes 98308
  14.0 187.9 %all-gather.5.cloned.1.call-start = ((), (), s32[]{:S(2)}) async-start(), calls=%async_computation.5 | async-start | bytes 6488064 | tf_op jit(solution)/shard_map/all_gather | solution.py:82
  14.2 6.8 %copy-start.15 = (f32[32,24]{1,0:T(8,128)}, f32[32,24]{1,0:T(8,128)S(1)}, u32[]{:S(2)}) copy-start(f32[32,24]{1,0:T(8,128)S(1)} %broadcast_multiply_fusion.2) | copy-start | bytes 9220
  14.6 6.4 %copy-start.19 = (f32[32,24]{1,0:T(8,128)}, f32[32,24]{1,0:T(8,128)S(1)}, u32[]{:S(2)}) copy-start(f32[32,24]{1,0:T(8,128)S(1)} %add_rsqrt_fusion) | copy-start | bytes 9220
  15.0 0.9 copy-start.5
  16.8 315.8 %reduce-scatter.6.cloned.1.call-start = ((), (), s32[]{:S(2)}) async-start(), calls=%async_computation.6 | async-start | bytes 7864320 | tf_op jit(solution)/shard_map/reduce_scatter | solution.py:14
  17.7 0.6 copy-start.17
  18.7 0.7 copy-start.9
  243.7 10.4 %copy-start.3 = (f32[32,16,128]{0,1,2:T(8,128)S(1)}, f32[32,16,128]{0,1,2:T(8,128)}, u32[]{:S(2)}) copy-start(f32[32,16,128]{0,1,2:T(8,128)} %copy.77) | copy-start | bytes 786436
  243.7 10.4 %copy-start.35 = (f32[128]{0:T(128)S(1)}, f32[128]{0:T(128)}, u32[]{:S(2)}) copy-start(f32[128]{0:T(128)} %param.22) | copy-start | bytes 1540
  253.9 0.7 copy-start.36
  255.8 0.8 copy-start.4
  288.7 44.2 %copy-start.11 = (bf16[32,16,128]{0,1,2:T(8,128)(2,1)S(1)}, bf16[32,16,128]{0,1,2:T(8,128)(2,1)}, u32[]{:S(2)}) copy-start(bf16[32,16,128]{0,1,2:T(8,128)(2,1)} %get-tuple-element.15) | copy-start | bytes 393220
  288.7 44.8 %copy-start.10 = (f32[32,16,128]{2,1,0:T(8,128)S(1)}, f32[32,16,128]{2,1,0:T(8,128)}, u32[]{:S(2)}) copy-start(f32[32,16,128]{2,1,0:T(8,128)} %copy-done.9) | copy-start | bytes 786436
  288.7 44.8 %copy-start.24 = (bf16[128,128]{1,0:T(8,128)(2,1)S(1)}, bf16[128,128]{1,0:T(8,128)(2,1)}, u32[]{:S(2)}) copy-start(bf16[128,128]{1,0:T(8,128)(2,1)} %param.19) | copy-start | bytes 98308
  288.7 45.6 %copy-start.14 = (bf16[32,16,128]{2,1,0:T(8,128)(2,1)S(1)}, bf16[32,16,128]{2,1,0:T(8,128)(2,1)}, u32[]{:S(2)}) copy-start(bf16[32,16,128]{2,1,0:T(8,128)(2,1)} %param.15) | copy-start | bytes 393220
  288.7 45.6 %copy-start.18 = (f32[32,16]{1,0:T(8,128)S(1)}, f32[32,16]{1,0:T(8,128)}, u32[]{:S(2)}) copy-start(f32[32,16]{1,0:T(8,128)} %copy-done.17) | copy-start | bytes 6148
  288.7 45.6 %copy-start.30 = (bf16[128,128]{1,0:T(8,128)(2,1)S(1)}, bf16[128,128]{1,0:T(8,128)(2,1)}, u32[]{:S(2)}) copy-start(bf16[128,128]{1,0:T(8,128)(2,1)} %param.18) | copy-start | bytes 98308
  288.7 45.6 %copy-start.32 = (f32[128]{0:T(128)S(1)}, f32[128]{0:T(128)}, u32[]{:S(2)}) copy-start(f32[128]{0:T(128)} %param.20) | copy-start | bytes 1540
  288.7 77.2 %all-to-all-start = ((bf16[8,96,16,128]{3,2,1,0:T(8,128)(2,1)}), bf16[8,96,16,128]{3,2,1,0:T(8,128)(2,1)}, u32[]{:S(2)}, u32[]{:S(2)}) async-start(bf16[8,96,16,128]{3,2,1,0:T(8,128)(2,1)} %bitcast.75), calls=%async_computation.2 | async-start | bytes 6291456 | tf_op jit(solution)/shard_map/all_to_all | solution.py:25
  295.2 74.3 %reduce-scatter.8.cloned.1.call-start = ((), (), s32[]{:S(2)}) async-start(), calls=%async_computation.7 | async-start | bytes 1966080 | tf_op jit(solution)/shard_map/reduce_scatter | solution.py:14
  332.6 59.9 %reduce-scatter.10.cloned.1.call-start = ((), (), s32[]{:S(2)}) async-start(), calls=%async_computation.8 | async-start | bytes 589824
  333.4 34.9 %copy-start.2 = (f32[16,96,256]{2,1,0:T(8,128)S(1)}, f32[16,96,256]{2,1,0:T(8,128)}, u32[]{:S(2)}) copy-start(f32[16,96,256]{2,1,0:T(8,128)} %copy-done.1) | copy-start | bytes 4718596
  368.3 3.2 copy-start.7
  368.3 3.2 copy-start.22
  368.3 3.2 copy-start.26
  368.3 3.2 copy-start.33
  369.5 23.0 %copy-start.6 = (f32[32,24,256]{2,1,0:T(8,128)S(1)}, f32[32,24,256]{2,1,0:T(8,128)}, u32[]{:S(2)}) copy-start(f32[32,24,256]{2,1,0:T(8,128)} %copy-done.5) | copy-start | bytes 2359300
  371.5 22.1 %copy-start.16 = (f32[32,24]{1,0:T(8,128)S(1)}, f32[32,24]{1,0:T(8,128)}, u32[]{:S(2)}) copy-start(f32[32,24]{1,0:T(8,128)} %copy-done.15) | copy-start | bytes 9220
  371.5 22.2 %copy-start.20 = (f32[32,24]{1,0:T(8,128)S(1)}, f32[32,24]{1,0:T(8,128)}, u32[]{:S(2)}) copy-start(f32[32,24]{1,0:T(8,128)} %copy-done.19) | copy-start | bytes 9220
  371.5 22.2 %copy-start.28 = (bf16[128,256]{1,0:T(8,128)(2,1)S(1)}, bf16[128,256]{1,0:T(8,128)(2,1)}, u32[]{:S(2)}) copy-start(bf16[128,256]{1,0:T(8,128)(2,1)} %param.16) | copy-start | bytes 196612
Sparse Core Ops, SparseCore 0:
  14.1 46.4 all-gather.2
  64.3 137.5 all-gather.4
  270.8 61.7 reduce-scatter.5
  335.0 27.1 reduce-scatter.7
  371.6 20.8 reduce-scatter.9
where the time goes:
time: 403 us; the launch traced here: 402 us
  waiting for transfers between devices  262 us (65%)
  local copies, waits for them, and re-layouts  68.1 us (17%)
  matrix products  35.1 us (9%)
  other arithmetic  15.8 us (4%)
  between operations  14.3 us (4%)
  starting transfers between devices  7.09 us (2%)
    all_gather x1, waiting for transfers between devices, shards(): left_whole = lax.all_gather(left, JA, axis=1, tiled=True)  137 us
    all_gather x1, local copies, waits for them, and re-layouts, shards(): left_whole = lax.all_gather(left, JA, axis=1, tiled=True)  41.8 us
    all_gather x1, waiting for transfers between devices, shards(): panel_piece = lax.all_gather(right, 'ia', axis=1, tiled=True)  39.5 us
    reduce_scatter x2, waiting for transfers between devices, summed_rows(): total = lax.psum_scatter(total, axis, scatter_dimension=0, tiled=True)  37.4 us
    all_to_all x1, waiting for transfers between devices, sent_and_summed(): lax.all_to_all(in_blocks(array, dim, devices), axis, 0, 0, tiled=True)  29.9 us
    unnamed x6, waiting for transfers between devices  17.3 us
    dot_general x1, matrix products, shards(): jnp.einsum('ijc,ikc->kjc', grad_tri, left_slice, preferred_element_type=j...  14 us
    dot_general x1, matrix products, shards(): jnp.einsum('ikc,jkc->ijc', left_slice, panel_piece, preferred_element_typ...  10.1 us
  transfers between devices with their start and end apart: 6, of which 5 were waited for; matrix products, arithmetic and copies ran while one was open for 9% of the time, Pallas kernels for 0%

commit v1 on v0

--- a/solution.py
+++ b/solution.py
@@ -79,7 +79,9 @@
     right, lin_right, sig_right, scaled_right, inv_right = project(
         column_rows, weights_right, input_gain, input_bias
     )
-    left_whole = lax.all_gather(left, JA, axis=1, tiled=True)
+    left_whole = jnp.concatenate(
+        lax.all_to_all(jnp.stack([left] * lax.axis_size(JA)), JA, 0, 0), axis=1
+    )
     panel_piece = lax.all_gather(right, "ia", axis=1, tiled=True)
     left_slice = left_whole
     running = jnp.einsum(

time: 403 us -> 374 us (0.928)
  starting transfers between devices: 7.09 us -> 55.3 us
  waiting for transfers between devices: 262 us -> 225 us
  local copies, waits for them, and re-layouts: 68.1 us -> 45.4 us
  matrix products: 35.1 us -> 18.3 us
    all_gather x1 -> x0, waiting for transfers between devices: 137 us -> none  [shards(): left_whole = lax.all_gather(left, JA, axis=1, tiled=True)]
    all_gather x1, waiting for transfers between devices: 39.5 us -> 106 us  [shards(): panel_piece = lax.all_gather(right, 'ia', axis=1, tiled=True)]
    all_gather x1 -> x0, local copies, waits for them, and re-layouts: 41.8 us -> none  [shards(): left_whole = lax.all_gather(left, JA, axis=1, tiled=True)]
    all_to_all x1, starting transfers between devices: 6.53 us -> 40 us  [sent_and_summed(): lax.all_to_all(in_blocks(array, dim, devices), axis, 0, 0, tiled=True)]
    all_to_all x0 -> x1, waiting for transfers between devices: none -> 23.2 us  [shards(): lax.all_to_all(jnp.stack([left] * lax.axis_size(JA)), JA, 0, 0)]
    all_to_all x0 -> x1, starting transfers between devices: none -> 14.7 us  [shards(): lax.all_to_all(jnp.stack([left] * lax.axis_size(JA)), JA, 0, 0)]
    reduce_scatter x2, waiting for transfers between devices: 37.4 us -> 51.2 us  [summed_rows(): total = lax.psum_scatter(total, axis, scatter_dimension=0, tiled=True)]
    all_to_all x1, waiting for transfers between devices: 29.9 us -> 19.8 us  [sent_and_summed(): lax.all_to_all(in_blocks(array, dim, devices), axis, 0, 0, tiled=True)]
  transfers between devices with their start and end apart: 6 -> 6, of which waited for: 5 -> 6; matrix products, arithmetic and copies ran while one was open for 9% -> 7% of each run, Pallas kernels for 0% -> 0%
where the time goes in v1:
time: 374 us; the launch traced here: 373 us
  waiting for transfers between devices  225 us (60%)
  starting transfers between devices  55.3 us (15%)
  local copies, waits for them, and re-layouts  45.4 us (12%)
  matrix products  18.3 us (5%)
  other arithmetic  14.3 us (4%)
  between operations  14.2 us (4%)
    all_gather x1, waiting for transfers between devices, shards(): panel_piece = lax.all_gather(right, 'ia', axis=1, tiled=True)  106 us
    reduce_scatter x2, waiting for transfers between devices, summed_rows(): total = lax.psum_scatter(total, axis, scatter_dimension=0, tiled=True)  51.2 us
    all_to_all x1, starting transfers between devices, sent_and_summed(): lax.all_to_all(in_blocks(array, dim, devices), axis, 0, 0, tiled=True)  40 us
    unnamed x5, waiting for transfers between devices  25 us
    all_to_all x1, waiting for transfers between devices, shards(): lax.all_to_all(jnp.stack([left] * lax.axis_size(JA)), JA, 0, 0)  23.2 us
    all_to_all x1, waiting for transfers between devices, sent_and_summed(): lax.all_to_all(in_blocks(array, dim, devices), axis, 0, 0, tiled=True)  19.8 us
    all_to_all x1, starting transfers between devices, shards(): lax.all_to_all(jnp.stack([left] * lax.axis_size(JA)), JA, 0, 0)  14.7 us
    convert_element_type x1, local copies, waits for them, and re-layouts, summed_rows(): total = terms.astype(jnp.bfloat16)  9.69 us
  transfers between devices with their start and end apart: 6, of which 6 were waited for; matrix products, arithmetic and copies ran while one was open for 7% of the time, Pallas kernels for 0%

profile of v1, /device:TPU:1, one launch (start us, length us, event | category | flops | bytes accessed | tf_op | source)
XLA Modules:
  0.0 372.9 jit_solution(15406798128972139360)
XLA Ops:
  7.2 1.1 convert_reduce_fusion.2
  8.3 1.2 fusion.36
  9.6 1.4 fusion.69
  11.0 0.9 copy-done.4
  12.0 4.1 %stack.2 = bf16[32,32,24,128]{3,2,1,0:T(8,128)(2,1)} broadcast(bf16[32,24,128]{2,1,0:T(8,128)(2,1)S(1)} %multiply_convert_fusion.2), dimensions={1,2,3} | broadcast | bytes 6488064 | tf_op jit(solution)/shard_map/stack | solution.py:83
  16.1 14.7 %all-to-all-start = ((bf16[32,32,24,128]{3,2,1,0:T(8,128)(2,1)}), bf16[32,32,24,128]{3,2,1,0:T(8,128)(2,1)}, u32[]{:S(2)}, u32[]{:S(2)}) async-start(bf16[32,32,24,128]{3,2,1,0:T(8,128)(2,1)} %stack.2), calls=%async_computation | async-start | bytes 12582912 | tf_op jit(solution)/shard_map/all_to_all | solution.py:83
  30.9 0.2 convert_reduce_fusion.1
  31.1 0.6 fusion.14
  31.8 0.6 fusion.37
  32.4 1.2 copy-done.1
  33.5 1.0 multiply_convert_fusion.1
  34.5 0.2 reduce-scatter.6.cloned.1.call-start
  35.0 0.2 fusion.64
  35.5 0.3 fusion.2
  35.8 0.2 fusion.76
  36.0 1.4 copy.79
  37.5 106.3 %all-gather.2.cloned.1.call-done = bf16[16,768,128]{2,1,0:T(8,128)(2,1)} async-done(((bf16[16,96,128]{2,1,0:T(8,128)(2,1)}), bf16[16,768,128]{2,1,0:T(8,128)(2,1)}) %all-gather.2.cloned.1.call-update) | async-done | bytes 3145744 | tf_op jit(solution)/shard_map/all_gather | solution.py:85
  143.7 3.9 %copy.76 = bf16[16,768,128]{1,0,2:T(8,128)(2,1)S(1)} copy(bf16[16,768,128]{2,1,0:T(8,128)(2,1)} %all-gather.2.cloned.1.call-done) | data formatting | bytes 6291456 | tf_op jit(solution)/shard_map/all_gather | solution.py:85
  147.7 23.2 %all-to-all-done = bf16[32,32,24,128]{3,2,1,0:T(8,128)(2,1)} async-done(((bf16[32,32,24,128]{3,2,1,0:T(8,128)(2,1)}), bf16[32,32,24,128]{3,2,1,0:T(8,128)(2,1)}, u32[]{:S(2)}, u32[]{:S(2)}) %all-to-all-start) | async-done | bytes 6291488 | tf_op jit(solution)/shard_map/all_to_all | solution.py:83
  170.9 7.2 %copy.75 = bf16[32,32,24,128]{3,2,0,1:T(8,128)(2,1)} copy(bf16[32,32,24,128]{3,2,1,0:T(8,128)(2,1)} %all-to-all-done) | data formatting | bytes 12582912 | tf_op jit(solution)/shard_map/all_to_all | solution.py:83
  178.1 9.0 %copy.77 = bf16[32,768,128]{1,0,2:T(8,128)(2,1)} copy(bf16[32,768,128]{2,1,0:T(8,128)(2,1)} %bitcast.78) | data formatting | bytes 12582912 | tf_op jit(solution)/shard_map/reshape | solution.py:82
  187.1 4.6 %fusion.99 = (f32[32,16]{0,1:T(8,128)S(1)}, f32[32,16,128]{0,1,2:T(8,128)S(1)}) fusion(bf16[16,768,128]{1,0,2:T(8,128)(2,1)S(1)} %copy.76, bf16[32,768,128]{1,0,2:T(8,128)(2,1)} %copy.77), kind=kOutput, calls=%fused_computation.142 | convolution fusion | flops 100728320 | bytes 9701376 | tf_op jit(solution)/shard_map/ikc,jkc->ijc/dot_general | solution.py:87
  191.8 0.2 multiply_reduce_fusion.1
  192.0 0.3 multiply_reduce_fusion.2
  192.4 1.2 multiply_convert_fusion
  193.7 0.8 copy-done.8
  194.5 4.4 %convert_bitcast_fusion = bf16[768,32,128]{0,1,2:T(8,128)(2,1)} fusion(bf16[16,768,128]{1,0,2:T(8,128)(2,1)S(1)} %copy.76, bf16[32,16,128]{0,1,2:T(8,128)(2,1)S(1)} %get-tuple-element.14), kind=kOutput, calls=%fused_computation.1 | convolution fusion | flops 103809024 | bytes 9568256 | tf_op jit(solution)/shard_map/ijc,jkc->kic/dot_general | solution.py:106
  198.9 9.7 %copy.81 = bf16[768,32,128]{2,1,0:T(8,128)(2,1)} copy(bf16[768,32,128]{0,1,2:T(8,128)(2,1)} %convert_bitcast_fusion) | data formatting | bytes 12582912 | tf_op jit(solution)/shard_map/convert_element_type | solution.py:12
  208.6 3.9 %convert_bitcast_fusion.1 = bf16[768,16,128]{0,1,2:T(8,128)(2,1)S(1)} fusion(bf16[32,16,128]{0,1,2:T(8,128)(2,1)} %copy-done.8, bf16[32,768,128]{1,0,2:T(8,128)(2,1)} %copy.77), kind=kOutput, calls=%fused_computation.2 | convolution fusion | flops 102236160 | bytes 9568256 | tf_op jit(solution)/shard_map/ijc,ikc->kjc/dot_general | solution.py:110
  212.6 4.0 %copy.84 = bf16[768,16,128]{2,1,0:T(8,128)(2,1)} copy(bf16[768,16,128]{0,1,2:T(8,128)(2,1)S(1)} %convert_bitcast_fusion.1) | data formatting | bytes 6291456 | tf_op jit(solution)/shard_map/convert_element_type | solution.py:110
  216.6 40.0 %all-to-all-start.1 = ((bf16[8,96,16,128]{3,2,1,0:T(8,128)(2,1)}), bf16[8,96,16,128]{3,2,1,0:T(8,128)(2,1)}, u32[]{:S(2)}, u32[]{:S(2)}) async-start(bf16[8,96,16,128]{3,2,1,0:T(8,128)(2,1)} %bitcast.79), calls=%async_computation.3 | async-start | bytes 6291456 | tf_op jit(solution)/shard_map/all_to_all | solution.py:25
  256.6 47.5 %reduce-scatter.6.cloned.1.call-done = bf16[192,32,128]{2,1,0:T(8,128)(2,1)} async-done(((bf16[768,32,128]{2,1,0:T(8,128)(2,1)}), bf16[192,32,128]{2,1,0:T(8,128)(2,1)}) %reduce-scatter.6.cloned.1.call-update) | async-done | bytes 1572880 | tf_op jit(solution)/shard_map/reduce_scatter | solution.py:14
  304.1 0.3 reduce-scatter.10.cloned.1.call-start
  304.4 0.5 copy.78
  305.0 0.8 multiply_convert_fusion.3
  305.8 0.4 fusion.98
  306.5 1.0 fusion.63
  307.5 19.8 %all-to-all-done.1 = bf16[8,96,16,128]{3,2,1,0:T(8,128)(2,1)} async-done(((bf16[8,96,16,128]{3,2,1,0:T(8,128)(2,1)}), bf16[8,96,16,128]{3,2,1,0:T(8,128)(2,1)}, u32[]{:S(2)}, u32[]{:S(2)}) %all-to-all-start.1) | async-done | bytes 3145760 | tf_op jit(solution)/shard_map/all_to_all | solution.py:25
  327.3 2.4 convert_reduce_fusion
  329.7 0.5 fusion.21
  330.2 3.6 reduce-scatter.8.cloned.1.call-done
  333.9 1.9 copy.99
  335.8 1.1 fusion.96
  336.9 1.7 fusion.13
  338.6 24.9 %reduce-scatter.10.cloned.1.call-done = bf16[24,4096]{1,0:T(8,128)(2,1)} async-done(((bf16[48,4096]{1,0:T(8,128)(2,1)}), bf16[24,4096]{1,0:T(8,128)(2,1)}) %reduce-scatter.10.cloned.1.call-update) | async-done | bytes 196624
  363.5 1.1 fusion.45
  364.6 0.5 fusion.97
  365.2 1.2 fusion.35
  (78 shorter events, 1.2 us)
Async XLA Ops:
  7.2 24.5 %copy-start = (bf16[128,256]{1,0:T(8,128)(2,1)S(1)}, bf16[128,256]{1,0:T(8,128)(2,1)}, u32[]{:S(2)}) copy-start(bf16[128,256]{1,0:T(8,128)(2,1)} %param.17) | copy-start | bytes 196612
  11.0 0.9 copy-start.4
  16.1 14.8 %copy-start.6 = (bf16[16,96,128]{2,1,0:T(8,128)(2,1)S(1)}, bf16[16,96,128]{2,1,0:T(8,128)(2,1)}, u32[]{:S(2)}) copy-start(bf16[16,96,128]{2,1,0:T(8,128)(2,1)} %param.13) | copy-start | bytes 1179652
  16.1 15.7 %copy-start.20 = (f32[128]{0:T(128)S(1)}, f32[128]{0:T(128)}, u32[]{:S(2)}) copy-start(f32[128]{0:T(128)} %param.20) | copy-start | bytes 1540
  16.1 15.7 %copy-start.22 = (f32[128]{0:T(128)S(1)}, f32[128]{0:T(128)}, u32[]{:S(2)}) copy-start(f32[128]{0:T(128)} %param.21) | copy-start | bytes 1540
  16.1 154.8 %all-to-all-start = ((bf16[32,32,24,128]{3,2,1,0:T(8,128)(2,1)}), bf16[32,32,24,128]{3,2,1,0:T(8,128)(2,1)}, u32[]{:S(2)}, u32[]{:S(2)}) async-start(bf16[32,32,24,128]{3,2,1,0:T(8,128)(2,1)} %stack.2), calls=%async_computation | async-start | bytes 12582912 | tf_op jit(solution)/shard_map/all_to_all | solution.py:83
  30.8 3.9 %copy-start.11 = (bf16[32,16,128]{2,1,0:T(8,128)(2,1)S(1)}, bf16[32,16,128]{2,1,0:T(8,128)(2,1)}, u32[]{:S(2)}) copy-start(bf16[32,16,128]{2,1,0:T(8,128)(2,1)} %param.14) | copy-start | bytes 393220
  30.8 4.6 %copy-start.18 = (bf16[128,128]{1,0:T(8,128)(2,1)S(1)}, bf16[128,128]{1,0:T(8,128)(2,1)}, u32[]{:S(2)}) copy-start(bf16[128,128]{1,0:T(8,128)(2,1)} %param.18) | copy-start | bytes 98308
  30.8 112.9 %all-gather.2.cloned.1.call-start = ((), (), s32[]{:S(2)}) async-start(), calls=%async_computation.5 | async-start | bytes 3538944 | tf_op jit(solution)/shard_map/all_gather | solution.py:85
  31.7 4.1 %copy-start.13 = (bf16[32,16,128]{2,1,0:T(8,128)(2,1)S(1)}, bf16[32,16,128]{2,1,0:T(8,128)(2,1)}, u32[]{:S(2)}) copy-start(bf16[32,16,128]{2,1,0:T(8,128)(2,1)} %param.15) | copy-start | bytes 393220
  31.7 4.1 %copy-start.15 = (bf16[128,128]{1,0:T(8,128)(2,1)S(1)}, bf16[128,128]{1,0:T(8,128)(2,1)}, u32[]{:S(2)}) copy-start(bf16[128,128]{1,0:T(8,128)(2,1)} %param.19) | copy-start | bytes 98308
  32.4 1.2 copy-start.1
  34.5 269.6 %reduce-scatter.6.cloned.1.call-start = ((), (), s32[]{:S(2)}) async-start(), calls=%async_computation.6 | async-start | bytes 7864320 | tf_op jit(solution)/shard_map/reduce_scatter | solution.py:14
  187.1 4.8 %copy-start.3 = (f32[32,16,128]{0,1,2:T(8,128)S(1)}, f32[32,16,128]{0,1,2:T(8,128)}, u32[]{:S(2)}) copy-start(f32[32,16,128]{0,1,2:T(8,128)} %copy.79) | copy-start | bytes 786436
  187.1 4.9 %copy-start.23 = (f32[128]{0:T(128)S(1)}, f32[128]{0:T(128)}, u32[]{:S(2)}) copy-start(f32[128]{0:T(128)} %param.22) | copy-start | bytes 1540
  191.7 0.7 copy-start.24
  193.7 0.8 copy-start.8
  216.5 87.9 %copy-start.10 = (bf16[32,16,128]{0,1,2:T(8,128)(2,1)S(1)}, bf16[32,16,128]{0,1,2:T(8,128)(2,1)}, u32[]{:S(2)}) copy-start(bf16[32,16,128]{0,1,2:T(8,128)(2,1)} %get-tuple-element.15) | copy-start | bytes 393220
  216.5 88.4 %copy-start.16 = (bf16[128,128]{1,0:T(8,128)(2,1)S(1)}, bf16[128,128]{1,0:T(8,128)(2,1)}, u32[]{:S(2)}) copy-start(bf16[128,128]{1,0:T(8,128)(2,1)} %param.19) | copy-start | bytes 98308
  216.5 89.3 %copy-start.12 = (bf16[32,16,128]{2,1,0:T(8,128)(2,1)S(1)}, bf16[32,16,128]{2,1,0:T(8,128)(2,1)}, u32[]{:S(2)}) copy-start(bf16[32,16,128]{2,1,0:T(8,128)(2,1)} %param.14) | copy-start | bytes 393220
  216.5 89.3 %copy-start.14 = (bf16[32,16,128]{2,1,0:T(8,128)(2,1)S(1)}, bf16[32,16,128]{2,1,0:T(8,128)(2,1)}, u32[]{:S(2)}) copy-start(bf16[32,16,128]{2,1,0:T(8,128)(2,1)} %param.15) | copy-start | bytes 393220
  216.5 89.3 %copy-start.19 = (bf16[128,128]{1,0:T(8,128)(2,1)S(1)}, bf16[128,128]{1,0:T(8,128)(2,1)}, u32[]{:S(2)}) copy-start(bf16[128,128]{1,0:T(8,128)(2,1)} %param.18) | copy-start | bytes 98308
  216.5 89.2 %copy-start.21 = (f32[128]{0:T(128)S(1)}, f32[128]{0:T(128)}, u32[]{:S(2)}) copy-start(f32[128]{0:T(128)} %param.20) | copy-start | bytes 1540
  216.6 110.7 %all-to-all-start.1 = ((bf16[8,96,16,128]{3,2,1,0:T(8,128)(2,1)}), bf16[8,96,16,128]{3,2,1,0:T(8,128)(2,1)}, u32[]{:S(2)}, u32[]{:S(2)}) async-start(bf16[8,96,16,128]{3,2,1,0:T(8,128)(2,1)} %bitcast.79), calls=%async_computation.3 | async-start | bytes 6291456 | tf_op jit(solution)/shard_map/all_to_all | solution.py:25
  256.6 77.3 %reduce-scatter.8.cloned.1.call-start = ((), (), s32[]{:S(2)}) async-start(), calls=%async_computation.7 | async-start | bytes 1966080 | tf_op jit(solution)/shard_map/reduce_scatter | solution.py:14
  304.1 59.3 %reduce-scatter.10.cloned.1.call-start = ((), (), s32[]{:S(2)}) async-start(), calls=%async_computation.8 | async-start | bytes 589824
  304.9 24.8 %copy-start.2 = (f32[16,96,256]{2,1,0:T(8,128)S(1)}, f32[16,96,256]{2,1,0:T(8,128)}, u32[]{:S(2)}) copy-start(f32[16,96,256]{2,1,0:T(8,128)} %copy-done.1) | copy-start | bytes 4718596
  329.7 6.1 %copy-start.7 = (bf16[16,96,128]{2,1,0:T(8,128)(2,1)S(1)}, bf16[16,96,128]{2,1,0:T(8,128)(2,1)}, u32[]{:S(2)}) copy-start(bf16[16,96,128]{2,1,0:T(8,128)(2,1)} %param.13) | copy-start | bytes 1179652
  330.2 33.3 %copy-start.5 = (f32[32,24,256]{2,1,0:T(8,128)S(1)}, f32[32,24,256]{2,1,0:T(8,128)}, u32[]{:S(2)}) copy-start(f32[32,24,256]{2,1,0:T(8,128)} %copy-done.4) | copy-start | bytes 2359300
  335.8 28.8 %copy-start.9 = (bf16[32,24,128]{2,1,0:T(8,128)(2,1)S(1)}, bf16[32,24,128]{2,1,0:T(8,128)(2,1)}, u32[]{:S(2)}) copy-start(bf16[32,24,128]{2,1,0:T(8,128)(2,1)} %param.12) | copy-start | bytes 589828
  335.8 28.8 %copy-start.17 = (bf16[128,256]{1,0:T(8,128)(2,1)S(1)}, bf16[128,256]{1,0:T(8,128)(2,1)}, u32[]{:S(2)}) copy-start(bf16[128,256]{1,0:T(8,128)(2,1)} %param.16) | copy-start | bytes 196612
Sparse Core Ops, SparseCore 0:
  34.6 109.0 all-gather.1
  208.7 95.3 reduce-scatter.5
  306.7 27.1 reduce-scatter.7
  336.2 27.2 reduce-scatter.9
